TPU v7x, 256 devices: a whole 4x4x8 slice. The times are simulated.
256 devices in a mesh: dp: 16 (over z, core), fsdp: 16 (over y, x).
Axes of the slice: x: 4, y: 4, z: 8, core: 2. Of those that a mesh axis runs over, the one named last changes fastest.
Arguments:
- hidden_in: bfloat16 [2048, 2304], P(('dp', 'fsdp')), may hold values from -30 to 30
- cache_pool: bfloat16 [8448, 16, 2, 2048], P('dp', None, None, 'fsdp'), may hold values from -64 to 64
- project_in: bfloat16 [2304, 3, 2048], P('dp', None, 'fsdp'), may hold values from -0.125 to 0.125
- project_out: bfloat16 [2048, 2304], P('fsdp', 'dp'), may hold values from -0.125 to 0.125
- norm_first: bfloat16 [2304], replicated, may hold values from 0.099609375 to 1.8984375
- norm_second: bfloat16 [2304], replicated, may hold values from 0.099609375 to 1.8984375
- router: bfloat16 [2304, 8], replicated, may hold values from -0.125 to 0.125
- gate_up: bfloat16 [8, 2304, 2, 5760], P(None, 'dp', None, 'fsdp'), may hold values from -0.125 to 0.125
- expert_down: bfloat16 [8, 2304, 5760], P(None, 'dp', 'fsdp'), may hold values from -0.078125 to 0.078125
- lengths: int32 [2048], replicated, may hold values from 65 to 128, as said below
- prompt_pages: int32 [64, 4], P('dp'), may hold values from 0 to 527, as said below
- own_pages: int32 [2048, 4], P('dp'), may hold values from 0 to 527, as said below
- groups: int32 [2048], P('dp'), may hold values from 0 to 3
- move_target: int32 [16, 8], replicated, may hold values from 0 to 15, as said below
- routes: int32 [2048, 2], P(('dp', 'fsdp')), may hold values from 0 to 7, all different within a row; in each aligned block of 8 rows (0 to 7, 8 to 15, ...) at most 4 rows name the same one
Outputs:
- layer_out: bfloat16 [2048, 2304], P(('dp', 'fsdp'))
Inputs may be any that keep to these rules, and one draw needn't show every extreme that they name: `lengths`: every request's cache holds its shared prompt's 4 * 16 positions and at least one more; some request holds 128. `prompt_pages`: within a row, the prompt pages of all its shared prompts and the own pages of all its requests are distinct pages. `own_pages`: within a row, the prompt pages of all its shared prompts and the own pages of all its requests are distinct pages. Row s sends its request slots 128 - 8 + j, j < 8, to rows move_target[s, j]; a row's 8 destinations are distinct and differ from s, and for each j every row is the destination of exactly one row. `routes`: in the 8 rows of one device no expert is named more than 4 times.
All inputs are finite; a program needn't handle non-finite values.
Results may differ from a plain program's by a relative error of at most 0.009.
Values may be sent and summed in bfloat16 or wider, within the bound.
A program may use at most 128 MiB of HBM per device.

v0:
```python
import jax
import jax.numpy as jnp
from jax import lax
from jax.sharding import PartitionSpec as P

HD = 64
CAP = 4


def rms_scale(values, scaling):
    return (
        values
        * lax.rsqrt(jnp.mean(values * values, axis=-1, keepdims=True) + 1e-06)
        * scaling.astype(jnp.float32)
    )


def rotate(tensor, position):
    half_dim = tensor.shape[-1] // 2
    channel = jnp.arange(half_dim, dtype=jnp.float32)
    inverse = jnp.exp(-jnp.log(10000.0) * 2.0 * channel / tensor.shape[-1])
    angles = position.astype(jnp.float32)[:, None, None] * inverse
    cosine = jnp.cos(angles)
    sine_part = jnp.sin(angles)
    first_half = tensor[..., :half_dim]
    second_half = tensor[..., half_dim:]
    return jnp.concatenate(
        [
            first_half * cosine - second_half * sine_part,
            second_half * cosine + first_half * sine_part,
        ],
        axis=-1,
    )


def local(
    hidden_in,
    cache_pool,
    project_in,
    project_out,
    norm_first,
    norm_second,
    router,
    gate_up,
    expert_down,
    lengths,
    prompt_pages,
    own_pages,
    groups,
    move_target,
    routes,
):
    rows_count = lax.axis_size("dp")
    fsdp_count = lax.axis_size("fsdp")
    my_row = lax.axis_index("dp")
    my_column = lax.axis_index("fsdp")
    req_local = hidden_in.shape[0]
    model_width = hidden_in.shape[1]
    req_row = req_local * fsdp_count
    movers = move_target.shape[1]
    staying = req_row - movers
    page_len = cache_pool.shape[1]
    head_cols = cache_pool.shape[3]
    heads_here = head_cols // HD
    span_total = (prompt_pages.shape[1] + own_pages.shape[1]) * page_len
    expert_count = router.shape[1]
    rows_per_expert = rows_count // expert_count
    slots_row = (CAP + rows_per_expert - 1) // rows_per_expert
    gate_send = jnp.repeat(gate_up, rows_per_expert, axis=0)
    down_send = jnp.repeat(expert_down, rows_per_expert, axis=0)
    row_tokens = lax.all_gather(hidden_in, "fsdp", axis=0, tiled=True)
    group_hit = (
        groups[:, None] == jnp.arange(prompt_pages.shape[0], dtype=jnp.int32)[None, :]
    ).astype(jnp.int32)
    prompt_list = jnp.sum(group_hit[:, :, None] * prompt_pages[None, :, :], axis=1)
    page_list = jnp.concatenate([prompt_list, own_pages], axis=1)
    mover_cache = cache_pool[page_list[staying:]]
    my_targets = move_target[my_row]
    send_select = (my_targets[:, None] == jnp.arange(rows_count, dtype=jnp.int32)[None, :]).astype(
        jnp.bfloat16
    )
    cache_send = jnp.einsum(
        "jd,jpqkc->dpqkc", send_select, mover_cache, preferred_element_type=jnp.float32
    ).astype(jnp.bfloat16)
    tokens_send = jnp.einsum(
        "jd,jc->dc", send_select, row_tokens[staying:], preferred_element_type=jnp.float32
    ).astype(jnp.bfloat16)
    cache_recv, tokens_recv = (
        lax.all_to_all(cache_send, "dp", split_axis=0, concat_axis=0, tiled=True),
        lax.all_to_all(tokens_send, "dp", split_axis=0, concat_axis=0, tiled=True),
    )
    arrive_hit = move_target == my_row
    arrive_select = arrive_hit.astype(jnp.bfloat16)
    arrived_cache = jnp.einsum(
        "sj,spqkc->jpqkc", arrive_select, cache_recv, preferred_element_type=jnp.float32
    ).astype(jnp.bfloat16)
    arrived_tokens = jnp.einsum(
        "sj,sc->jc", arrive_select, tokens_recv, preferred_element_type=jnp.float32
    ).astype(jnp.bfloat16)
    source_row = jnp.sum(
        arrive_hit.astype(jnp.int32) * jnp.arange(rows_count, dtype=jnp.int32)[:, None], axis=0
    )
    row_lengths = lax.dynamic_slice_in_dim(lengths, my_row * req_row, req_row)
    arrived_lengths = lengths[source_row * req_row + staying + jnp.arange(movers, dtype=jnp.int32)]
    position = jnp.concatenate([row_lengths[:staying], arrived_lengths])
    tokens_row = jnp.concatenate([row_tokens[:staying], arrived_tokens], axis=0)
    normed_attn = rms_scale(tokens_row.astype(jnp.float32), norm_first).astype(jnp.bfloat16)
    piece = lax.all_gather(project_in, "dp", axis=0, tiled=True)
    projected = jnp.dot(
        normed_attn,
        piece.reshape(piece.shape[0], 3 * head_cols),
        preferred_element_type=jnp.float32,
    )
    projected = projected.reshape(req_row, 3, heads_here, HD)
    query = rotate(projected[:, 0], position).astype(jnp.bfloat16)
    key_new = rotate(projected[:, 1], position).astype(jnp.bfloat16)
    value_new = projected[:, 2].astype(jnp.bfloat16)
    resident_cache = cache_pool[page_list[:staying]]
    cache_rows = jnp.concatenate([resident_cache, arrived_cache], axis=0).reshape(
        req_row, span_total, 2, heads_here, HD
    )
    key_rows = cache_rows[:, :, 0]
    value_rows = cache_rows[:, :, 1]
    scale_factor = HD ** (-0.5)
    scores = (
        jnp.einsum("nhd,nlhd->nhl", query, key_rows, preferred_element_type=jnp.float32)
        * scale_factor
    )
    valid_mask = jnp.arange(span_total, dtype=jnp.int32)[None, :] < position[:, None]
    scores = jnp.where(valid_mask[:, None, :], scores, -jnp.inf)
    own_score = (
        jnp.sum(query.astype(jnp.float32) * key_new.astype(jnp.float32), axis=-1) * scale_factor
    )
    highest = jnp.maximum(jnp.max(scores, axis=-1), own_score)
    weights_cache = jnp.exp(scores - highest[..., None])
    weight_own = jnp.exp(own_score - highest)
    denominator = jnp.sum(weights_cache, axis=-1) + weight_own
    probs_cache = (weights_cache / denominator[..., None]).astype(jnp.bfloat16)
    prob_own = (weight_own / denominator).astype(jnp.bfloat16)
    mixture = jnp.einsum(
        "nhl,nlhd->nhd", probs_cache, value_rows, preferred_element_type=jnp.float32
    )
    mixture = mixture + prob_own.astype(jnp.float32)[..., None] * value_new.astype(jnp.float32)
    heads_out = mixture.astype(jnp.bfloat16).reshape(req_row, head_cols)
    out_columns = lax.all_gather(project_out, "dp", axis=1, tiled=True)
    attn_proj = lax.psum_scatter(
        jnp.dot(heads_out, out_columns, preferred_element_type=jnp.float32),
        "fsdp",
        scatter_dimension=0,
        tiled=True,
    )
    mine_tokens = lax.dynamic_slice_in_dim(tokens_row, my_column * req_local, req_local, 0)
    resid = mine_tokens.astype(jnp.float32) + attn_proj
    moe_in = rms_scale(resid, norm_second).astype(jnp.bfloat16)
    logits = jnp.dot(moe_in, router, preferred_element_type=jnp.float32)
    expert_ids = jnp.arange(expert_count, dtype=jnp.int32)
    picked = routes[:, :, None] == expert_ids[None, None, :]
    chosen = jnp.sum(jnp.where(picked, logits[:, None, :], 0.0), axis=-1)
    weight_pair = jnp.stack(
        [jax.nn.sigmoid(chosen[:, 0] - chosen[:, 1]), jax.nn.sigmoid(chosen[:, 1] - chosen[:, 0])],
        axis=1,
    )
    mix_expert = jnp.sum(picked.astype(jnp.float32) * weight_pair[:, :, None], axis=1)
    member = jnp.sum(picked.astype(jnp.int32), axis=1)
    rank_expert = jnp.cumsum(member, axis=0) - member
    row_numbers = jnp.arange(rows_count, dtype=jnp.int32)
    expert_of_row = (row_numbers[:, None] // rows_per_expert == expert_ids[None, :]).astype(
        jnp.int32
    )
    replica_of_row = row_numbers % rows_per_expert
    member_row = jnp.sum(member[:, None, :] * expert_of_row[None, :, :], axis=-1)
    rank_row = jnp.sum(rank_expert[:, None, :] * expert_of_row[None, :, :], axis=-1)
    mix_row = jnp.sum(
        mix_expert[:, None, :] * expert_of_row[None, :, :].astype(jnp.float32), axis=-1
    )
    slot_ids = jnp.arange(slots_row, dtype=jnp.int32)
    wanted_rank = slot_ids[None, :, None] * rows_per_expert + replica_of_row[:, None, None]
    select = (member_row.T[:, None, :] == 1) & (rank_row.T[:, None, :] == wanted_rank)
    dispatch = jnp.einsum(
        "dst,tm->dsm", select.astype(jnp.bfloat16), moe_in, preferred_element_type=jnp.float32
    ).astype(jnp.bfloat16)
    received = lax.all_to_all(dispatch, "dp", split_axis=0, concat_axis=0, tiled=True)
    expert_tokens = lax.all_gather(received[None], "fsdp", axis=0, tiled=True)
    gate_whole, down_whole = (
        lax.all_to_all(gate_send, "dp", split_axis=0, concat_axis=1, tiled=True),
        lax.all_to_all(down_send, "dp", split_axis=0, concat_axis=1, tiled=True),
    )
    flattened = expert_tokens.reshape(-1, model_width)
    units_here = gate_up.shape[3]
    gate_cols = gate_whole[0].reshape(model_width, 2 * units_here)
    down_cols = down_whole[0]
    both_parts = jnp.dot(flattened, gate_cols, preferred_element_type=jnp.float32)
    activation = (jax.nn.silu(both_parts[:, :units_here]) * both_parts[:, units_here:]).astype(
        jnp.bfloat16
    )
    returned = lax.psum_scatter(
        lax.dot_general(
            activation, down_cols, (((1,), (1,)), ((), ())), preferred_element_type=jnp.float32
        ).astype(jnp.bfloat16),
        "fsdp",
        scatter_dimension=0,
        tiled=True,
    ).astype(jnp.float32)
    back_rows = lax.all_to_all(
        returned.reshape(rows_count, slots_row, model_width),
        "dp",
        split_axis=0,
        concat_axis=0,
        tiled=True,
    )
    coefficient = select.astype(jnp.float32) * mix_row.T[:, None, :]
    moe_total = jnp.einsum("dst,dsm->tm", coefficient, back_rows, precision=lax.Precision.HIGHEST)
    return (resid + moe_total).astype(jnp.bfloat16)


def solution(mesh):
    placed = (
        P(("dp", "fsdp"), None),
        P("dp", None, None, "fsdp"),
        P("dp", None, "fsdp"),
        P("fsdp", "dp"),
        P(),
        P(),
        P(),
        P(None, "dp", None, "fsdp"),
        P(None, "dp", "fsdp"),
        P(),
        P("dp", None),
        P("dp", None),
        P("dp"),
        P(),
        P(("dp", "fsdp"), None),
    )
    return jax.shard_map(
        local, mesh=mesh, in_specs=placed, out_specs=P(("dp", "fsdp"), None), check_vma=False
    )
```

profile of v0, /device:TPU:1, one launch (start us, length us, event | category | flops | bytes accessed | tf_op | source)
XLA Modules:
  0.0 533.4 jit_solution(7687817300184575141)
XLA Ops:
  6.5 0.7 all-gather.4.cloned.1.call-update
  7.3 20.2 %all_gather.12 = bf16[128,2304]{1,0:T(8,128)(2,1)S(1)} all-gather(bf16[8,2304]{1,0:T(8,128)(2,1)} %param.15), channel_id=1, replica_groups=mesh['dp'=16,'fsdp'=16] {'fsdp'}, dimensions={0}, use_global_device_ids=true | all-gather | bytes 626688 | tf_op jit(solution)/shard_map/all_gather | solution.py:71
  27.5 0.9 dynamic-slice_reduce_fusion
  28.3 0.3 fusion
  28.6 0.5 broadcast.327
  29.1 0.7 reduce.6
  29.8 0.6 reshape.422
  30.5 14.2 %all-to-all-start = ((bf16[16,2,1152]{2,1,0:T(2,128)(2,1)}), bf16[16,2,1152]{2,1,0:T(2,128)(2,1)S(1)}, u32[]{:S(2)}, u32[]{:S(2)}) async-start(bf16[16,2,1152]{2,1,0:T(2,128)(2,1)} %reshape.422), calls=%async_computation | async-start | bytes 147456 | tf_op jit(solution)/shard_map/all_to_all | solution.py:90
  44.7 0.7 fusion.43
  45.3 0.8 multiply_reduce_fusion.7
  46.1 0.7 pad_add_fusion
  47.0 3.8 gather_fusion.2
  50.9 0.6 convolution_convert_fusion.4
  51.5 1.9 copy.108
  53.5 0.1 copy.104
  53.7 27.4 %gather_fusion.1 = bf16[960,16,2,128]{3,2,1,0:T(2,128)(2,1)} fusion(bf16[528,16,2,128]{3,2,1,0:T(2,128)(2,1)} %param.16, s32[1024]{0:T(1024)S(1)} %pad_clamp_fusion.1), kind=kCustom, calls=%fused_computation.1 | custom fusion | bytes 15732480 | tf_op jit(solution)/shard_map/gather | solution.py:118
  81.0 7.4 %copy.105 = bf16[960,16,2,128]{3,1,2,0:T(8,128)(2,1)} copy(bf16[960,16,2,128]{3,2,1,0:T(2,128)(2,1)} %gather_fusion.1) | data formatting | bytes 15728640 | tf_op jit(solution)/shard_map/gather | solution.py:118
  88.4 7.4 %all-to-all-start.1 = ((bf16[16,8,16,2,128]{4,3,2,1,0:T(2,128)(2,1)}), bf16[16,8,16,2,128]{4,3,2,1,0:T(2,128)(2,1)S(1)}, u32[]{:S(2)}, u32[]{:S(2)}) async-start(bf16[16,8,16,2,128]{4,3,2,1,0:T(2,128)(2,1)} %copy.108), calls=%async_computation.1 | async-start | bytes 2097152 | tf_op jit(solution)/shard_map/all_to_all | solution.py:89
  95.9 0.1 select_reduce_fusion.2
  96.0 0.6 gather_fusion
  96.8 0.1 iota_compare_fusion
  96.9 0.1 multiply_cosine_fusion
  97.1 37.6 %all_gather.14 = bf16[128,2304]{0,1:T(8,128)(2,1)S(1)} all-gather(bf16[128,144]{0,1:T(8,128)(2,1)S(1)} %copy-done.3), channel_id=1, replica_groups=mesh['dp'=16,'fsdp'=16] {'dp'}, dimensions={1}, use_global_device_ids=true | all-gather | bytes 626688 | tf_op jit(solution)/shard_map/all_gather | solution.py:145
  134.8 0.1 convolution_convert_fusion.3
  134.9 0.2 fusion.3
  135.1 0.7 convolution_convert_fusion.5
  135.8 0.1 copy.110
  135.9 7.0 %pad_maximum_fusion = bf16[128,8,16,2,128]{4,2,3,1,0:T(8,128)(2,1)} fusion(bf16[8,8,16,2,128]{4,2,3,1,0:T(8,128)(2,1)S(1)} %copy.110, bf16[120,8,16,2,128]{4,2,3,1,0:T(8,128)(2,1)} %bitcast.84), kind=kLoop, calls=%fused_computation.3 | loop fusion | flops 4194304 | bytes 16777216 | tf_op jit(solution)/shard_map/concatenate | solution.py:119
  143.0 13.0 %copy.111 = bf16[128,8,16,2,128]{0,4,3,2,1:T(8,128)(2,1)} copy(bf16[128,8,16,2,128]{4,2,3,1,0:T(8,128)(2,1)} %pad_maximum_fusion) | data formatting | bytes 16777216 | tf_op jit(solution)/shard_map/concatenate | solution.py:119
  156.0 3.8 copy.103
  159.8 2.2 fusion.9
  162.0 3.9 multiply_reduce_fusion.1
  165.9 0.1 copy.123
  166.1 0.1 fusion.17
  166.2 0.2 fusion.18
  166.4 0.2 fusion.21
  166.6 0.1 copy.132
  166.7 3.3 multiply_reduce_fusion
  170.1 1.4 fusion.53
  171.6 0.6 dynamic-slice
  173.1 91.7 %all-reduce.3.cloned.1.call-done = f32[128,2304]{1,0:T(8,128)} async-done(((f32[128,2304]{1,0:T(8,128)}), f32[128,2304]{1,0:T(8,128)}) %all-reduce.3.cloned.1.call-update) | async-done | bytes 1179664
  264.8 1.0 multiply_reduce_fusion.2
  265.9 0.3 convolution_convert_fusion.1
  266.1 0.1 copy.112
  266.2 18.5 %all_to_all.45 = bf16[16,2,2304]{2,1,0:T(2,128)(2,1)} all-to-all(bf16[16,2,2304]{2,1,0:T(2,128)(2,1)S(1)} %copy.112), channel_id=1, replica_groups=mesh['dp'=16,'fsdp'=16] {'dp'}, dimensions={0} | all-to-all | bytes 294912 | tf_op jit(solution)/shard_map/all_to_all | solution.py:182
  284.7 5.1 broadcast_in_dim.37
  289.8 4.5 all-to-all-start.3
  294.4 0.7 all-gather.6.cloned.1.call-update
  295.1 78.4 %all-to-all-done.3 = bf16[16,144,2,360]{3,2,1,0:T(2,128)(2,1)} async-done(((bf16[16,144,2,360]{3,2,1,0:T(2,128)(2,1)}), bf16[16,144,2,360]{3,2,1,0:T(2,128)(2,1)}, u32[]{:S(2)}, u32[]{:S(2)}) %all-to-all-start.3) | async-done | bytes 3317792 | tf_op jit(solution)/shard_map/all_to_all | solution.py:185
  373.5 1.4 broadcast_in_dim.38
  374.9 5.5 %all-to-all-start.4 = ((bf16[16,144,360]{2,1,0:T(8,128)(2,1)}), bf16[16,144,360]{2,1,0:T(8,128)(2,1)}, u32[]{:S(2)}, u32[]{:S(2)}) async-start(bf16[16,144,360]{2,1,0:T(8,128)(2,1)} %bitcast.30), calls=%async_computation.4 | async-start | bytes 3538944 | tf_op jit(solution)/shard_map/all_to_all | solution.py:186
  380.4 0.3 reduce-scatter.2.cloned.1.call-start
  380.7 8.5 %reshape_squeeze.3 = bf16[2304,720]{1,0:T(8,128)(2,1)} reshape(bf16[16,144,2,360]{3,2,1,0:T(2,128)(2,1)} %all-to-all-done.3) | data formatting | bytes 6635520 | tf_op jit(solution)/shard_map/reshape;squeeze | solution.py:190
  389.2 4.9 reshape.373
  394.1 5.1 fusion.54
  399.2 23.7 %all-to-all-done.4 = bf16[16,144,360]{2,1,0:T(8,128)(2,1)} async-done(((bf16[16,144,360]{2,1,0:T(8,128)(2,1)}), bf16[16,144,360]{2,1,0:T(8,128)(2,1)}, u32[]{:S(2)}, u32[]{:S(2)}) %all-to-all-start.4) | async-done | bytes 1658912 | tf_op jit(solution)/shard_map/all_to_all | solution.py:186
  422.9 4.9 convolution_convert_fusion
  427.8 0.2 fusion.51
  428.0 0.2 select_reduce_fusion.1
  428.1 74.2 %reduce-scatter.2.cloned.1.call-done = bf16[32,2304]{1,0:T(8,128)(2,1)} async-done(((bf16[512,2304]{1,0:T(8,128)(2,1)}), bf16[32,2304]{1,0:T(8,128)(2,1)}) %reduce-scatter.2.cloned.1.call-update) | async-done | bytes 147472 | tf_op jit(solution)/shard_map/reduce_scatter | solution.py:196
  502.4 1.8 reshape.380
  504.1 9.4 %all-to-all-start.5 = ((f32[16,2,2304]{2,1,0:T(2,128)}), f32[16,2,2304]{2,1,0:T(2,128)S(1)}, u32[]{:S(2)}, u32[]{:S(2)}) async-start(f32[16,2,2304]{2,1,0:T(2,128)} %reshape.380), calls=%async_computation.6 | async-start | bytes 589824 | tf_op jit(solution)/shard_map/all_to_all | solution.py:204
  513.7 12.2 %all-to-all-done.5 = f32[16,2,2304]{2,1,0:T(2,128)S(1)} async-done(((f32[16,2,2304]{2,1,0:T(2,128)}), f32[16,2,2304]{2,1,0:T(2,128)S(1)}, u32[]{:S(2)}, u32[]{:S(2)}) %all-to-all-start.5) | async-done | bytes 294944 | tf_op jit(solution)/shard_map/all_to_all | solution.py:204
  525.9 0.9 fusion.2
  (66 shorter events, 1.4 us)
Async XLA Ops:
  6.5 421.2 %copy-start = (bf16[2304,8]{0,1:T(8,128)(2,1)S(1)}, bf16[2304,8]{0,1:T(8,128)(2,1)}, u32[]{:S(2)}) copy-start(bf16[2304,8]{0,1:T(8,128)(2,1)} %param.21) | copy-start | bytes 110596
  6.5 149.4 %all-gather.4.cloned.1.call-start = ((), (), s32[]{:S(2)}) async-start(), calls=%async_computation.7 | async-start | bytes 1880064 | tf_op jit(solution)/shard_map/all_gather | solution.py:108
  30.5 58.0 %all-to-all-start = ((bf16[16,2,1152]{2,1,0:T(2,128)(2,1)}), bf16[16,2,1152]{2,1,0:T(2,128)(2,1)S(1)}, u32[]{:S(2)}, u32[]{:S(2)}) async-start(bf16[16,2,1152]{2,1,0:T(2,128)(2,1)} %reshape.422), calls=%async_computation | async-start | bytes 147456 | tf_op jit(solution)/shard_map/all_to_all | solution.py:90
  81.0 7.4 %copy-start.6 = (bf16[2304]{0:T(1024)(128)(2,1)S(1)}, bf16[2304]{0:T(1024)(128)(2,1)}, u32[]{:S(2)}) copy-start(bf16[2304]{0:T(1024)(128)(2,1)} %param.19) | copy-start | bytes 13828
  81.0 14.8 %copy-start.4 = (s32[16,8]{0,1:T(8,128)S(1)}, s32[16,8]{0,1:T(8,128)}, u32[]{:S(2)}) copy-start(s32[16,8]{0,1:T(8,128)} %param.28) | copy-start | bytes 1540
  88.4 7.6 %copy-start.1 = (s32[2048]{0:T(1024)S(1)}, s32[2048]{0:T(1024)}, u32[]{:S(2)}) copy-start(s32[2048]{0:T(1024)} %param.24) | copy-start | bytes 24580
  88.4 8.6 %copy-start.3 = (bf16[128,144]{0,1:T(8,128)(2,1)S(1)}, bf16[128,144]{0,1:T(8,128)(2,1)}, u32[]{:S(2)}) copy-start(bf16[128,144]{0,1:T(8,128)(2,1)} %param.18) | copy-start | bytes 110596
  88.4 46.7 %all-to-all-start.1 = ((bf16[16,8,16,2,128]{4,3,2,1,0:T(2,128)(2,1)}), bf16[16,8,16,2,128]{4,3,2,1,0:T(2,128)(2,1)S(1)}, u32[]{:S(2)}, u32[]{:S(2)}) async-start(bf16[16,8,16,2,128]{4,3,2,1,0:T(2,128)(2,1)} %copy.108), calls=%async_computation.1 | async-start | bytes 2097152 | tf_op jit(solution)/shard_map/all_to_all | solution.py:89
  95.8 169.0 %all-reduce.3.cloned.1.call-start = ((), (), s32[]{:S(2)}) async-start(), calls=%async_computation.10 | async-start | bytes 2359296
  170.0 1.5 copy-start.5
  170.0 1.6 copy-start.7
  170.0 1.6 copy-start.8
  289.8 83.7 %copy-start.2 = (bf16[8,144,360]{2,1,0:T(8,128)(2,1)S(1)}, bf16[8,144,360]{2,1,0:T(8,128)(2,1)}, u32[]{:S(2)}) copy-start(bf16[8,144,360]{2,1,0:T(8,128)(2,1)} %param.23) | copy-start | bytes 2488324
  289.8 83.7 %all-to-all-start.3 = ((bf16[16,144,2,360]{3,2,1,0:T(2,128)(2,1)}), bf16[16,144,2,360]{3,2,1,0:T(2,128)(2,1)}, u32[]{:S(2)}, u32[]{:S(2)}) async-start(bf16[16,144,2,360]{3,2,1,0:T(2,128)(2,1)} %bitcast.85), calls=%async_computation.3 | async-start | bytes 7077888 | tf_op jit(solution)/shard_map/all_to_all | solution.py:185
  294.4 94.8 %all-gather.6.cloned.1.call-start = ((), (), s32[]{:S(2)}) async-start(), calls=%async_computation.9 | async-start | bytes 2506752 | tf_op jit(solution)/shard_map/all_gather | solution.py:183
  374.9 48.0 %all-to-all-start.4 = ((bf16[16,144,360]{2,1,0:T(8,128)(2,1)}), bf16[16,144,360]{2,1,0:T(8,128)(2,1)}, u32[]{:S(2)}, u32[]{:S(2)}) async-start(bf16[16,144,360]{2,1,0:T(8,128)(2,1)} %bitcast.30), calls=%async_computation.4 | async-start | bytes 3538944 | tf_op jit(solution)/shard_map/all_to_all | solution.py:186
  380.4 122.0 %reduce-scatter.2.cloned.1.call-start = ((), (), s32[]{:S(2)}) async-start(), calls=%async_computation.8 | async-start | bytes 2506752 | tf_op jit(solution)/shard_map/reduce_scatter | solution.py:196
  504.1 21.8 %all-to-all-start.5 = ((f32[16,2,2304]{2,1,0:T(2,128)}), f32[16,2,2304]{2,1,0:T(2,128)S(1)}, u32[]{:S(2)}, u32[]{:S(2)}) async-start(f32[16,2,2304]{2,1,0:T(2,128)} %reshape.380), calls=%async_computation.6 | async-start | bytes 589824 | tf_op jit(solution)/shard_map/all_to_all | solution.py:204
Sparse Core Ops, SparseCore 0:
  9.2 43.5 all-gather.3
  171.6 93.1 all-reduce.2
  297.6 48.1 all-gather.5
  427.9 74.4 reduce-scatter.1
where the time goes:
time: 535 us; the launch traced here: 533 us
  waiting for transfers between devices  282 us (53%)
  local copies, waits for them, and re-layouts  83.3 us (16%)
  blocking collectives  76.3 us (14%)
  starting transfers between devices  41.3 us (8%)
  other arithmetic  20 us (4%)
  matrix products  16.5 us (3%)
  between operations  14.2 us (3%)
    unnamed x5, waiting for transfers between devices  93.2 us
    all_to_all x1, waiting for transfers between devices, local(): lax.all_to_all(gate_send, 'dp', split_axis=0, concat_axis=1, tiled=True)  78.4 us
    reduce_scatter x1, waiting for transfers between devices, local(): lax.psum_scatter(lax.dot_general(activation, down_cols, (((1,), (1,)), ((...  74.2 us
    all_gather x1, blocking collectives, local(): out_columns = lax.all_gather(project_out, 'dp', axis=1, tiled=True)  37.6 us
    gather x2, local copies, waits for them, and re-layouts, local(): resident_cache = cache_pool[page_list[:staying]]  34.7 us
    all_to_all x1, waiting for transfers between devices, local(): lax.all_to_all(down_send, 'dp', split_axis=0, concat_axis=1, tiled=True)  23.7 us
    all_gather x1, blocking collectives, local(): row_tokens = lax.all_gather(hidden_in, 'fsdp', axis=0, tiled=True)  20.2 us
    all_to_all x1, blocking collectives, local(): lax.all_to_all(dispatch, 'dp', split_axis=0, concat_axis=0, tiled=True)  18.5 us
  transfers between devices with their start and end apart: 9, of which 5 were waited for; matrix products, arithmetic and copies ran while one was open for 17% of the time, Pallas kernels for 0%

commit v1 on v0

--- a/solution.py
+++ b/solution.py
@@ -5,6 +5,11 @@
 
 HD = 64
 CAP = 4
+
+
+def gather_over(shard, axis, dim):
+    repeated = jnp.stack([shard] * lax.axis_size(axis))
+    return jnp.concatenate(lax.all_to_all(repeated, axis, 0, 0), axis=dim)
 
 
 def rms_scale(values, scaling):
@@ -68,7 +73,7 @@
     slots_row = (CAP + rows_per_expert - 1) // rows_per_expert
     gate_send = jnp.repeat(gate_up, rows_per_expert, axis=0)
     down_send = jnp.repeat(expert_down, rows_per_expert, axis=0)
-    row_tokens = lax.all_gather(hidden_in, "fsdp", axis=0, tiled=True)
+    row_tokens = gather_over(hidden_in, "fsdp", 0)
     group_hit = (
         groups[:, None] == jnp.arange(prompt_pages.shape[0], dtype=jnp.int32)[None, :]
     ).astype(jnp.int32)

time: 535 us -> 507 us (0.948)
  blocking collectives: 76.3 us -> 37.3 us
  waiting for transfers between devices: 282 us -> 289 us
    all_gather x1 -> x0, blocking collectives: 20.2 us -> none  [local(): row_tokens = lax.all_gather(hidden_in, 'fsdp', axis=0, tiled=True)]
    all_gather x1, blocking collectives: 37.6 us -> 18.8 us  [local(): out_columns = lax.all_gather(project_out, 'dp', axis=1, tiled=True)]
    all_to_all x0 -> x1, starting transfers between devices: none -> 7.58 us  [gather_over(): return jnp.concatenate(lax.all_to_all(repeated, axis, 0, 0), axis=dim)]
    all_to_all x1, waiting for transfers between devices: 0.01 us -> 6.32 us  [local(): lax.all_to_all(tokens_send, 'dp', split_axis=0, concat_axis=0, tiled=True)]
  transfers between devices with their start and end apart: 9 -> 10, of which waited for: 5 -> 7; matrix products, arithmetic and copies ran while one was open for 17% -> 19% of each run, Pallas kernels for 0% -> 0%
where the time goes in v1:
time: 507 us; the launch traced here: 505 us
  waiting for transfers between devices  289 us (57%)
  local copies, waits for them, and re-layouts  86.4 us (17%)
  starting transfers between devices  41.5 us (8%)
  blocking collectives  37.3 us (7%)
  other arithmetic  20.5 us (4%)
  matrix products  16.5 us (3%)
  between operations  14.1 us (3%)
    unnamed x5, waiting for transfers between devices  93.6 us
    all_to_all x1, waiting for transfers between devices, local(): lax.all_to_all(gate_send, 'dp', split_axis=0, concat_axis=1, tiled=True)  78.4 us
    reduce_scatter x1, waiting for transfers between devices, local(): lax.psum_scatter(lax.dot_general(activation, down_cols, (((1,), (1,)), ((...  74.2 us
    gather x2, local copies, waits for them, and re-layouts, local(): resident_cache = cache_pool[page_list[:staying]]  34.7 us
    all_to_all x1, waiting for transfers between devices, local(): lax.all_to_all(down_send, 'dp', split_axis=0, concat_axis=1, tiled=True)  23.7 us
    all_gather x1, blocking collectives, local(): out_columns = lax.all_gather(project_out, 'dp', axis=1, tiled=True)  18.8 us
    all_to_all x1, blocking collectives, local(): lax.all_to_all(dispatch, 'dp', split_axis=0, concat_axis=0, tiled=True)  18.5 us
    concatenate x1, local copies, waits for them, and re-layouts, local(): jnp.concatenate([resident_cache, arrived_cache], axis=0)  13 us
  transfers between devices with their start and end apart: 10, of which 7 were waited for; matrix products, arithmetic and copies ran while one was open for 19% of the time, Pallas kernels for 0%

profile of v1, /device:TPU:1, one launch (start us, length us, event | category | flops | bytes accessed | tf_op | source)
XLA Modules:
  0.0 505.0 jit_solution(11663005182843686577)
XLA Ops:
  6.5 0.7 all-gather.4.cloned.1.call-update
  7.3 1.6 stack.4
  8.9 7.6 %all-to-all-start = ((bf16[16,8,2304]{2,1,0:T(8,128)(2,1)}), bf16[16,8,2304]{2,1,0:T(8,128)(2,1)S(1)}, u32[]{:S(2)}, u32[]{:S(2)}) async-start(bf16[16,8,2304]{2,1,0:T(8,128)(2,1)} %stack.4), calls=%async_computation | async-start | bytes 1179648 | tf_op jit(solution)/shard_map/all_to_all | solution.py:12
  16.5 0.7 fusion.42
  17.1 0.8 multiply_reduce_fusion.7
  17.9 0.7 pad_add_fusion
  18.8 0.8 select_reduce_fusion.2
  19.6 0.9 dynamic-slice_reduce_fusion
  20.5 1.3 gather_fusion
  21.8 0.8 dynamic_slice.11
  22.6 3.9 gather_fusion.2
  26.5 0.6 convolution_convert_fusion.4
  27.2 0.4 all-to-all-done
  27.5 0.3 fusion
  27.8 0.5 broadcast.329
  28.3 0.7 reduce.6
  29.0 0.6 reshape.427
  29.6 10.6 %all-to-all-start.1 = ((bf16[16,2,1152]{2,1,0:T(2,128)(2,1)}), bf16[16,2,1152]{2,1,0:T(2,128)(2,1)S(1)}, u32[]{:S(2)}, u32[]{:S(2)}) async-start(bf16[16,2,1152]{2,1,0:T(2,128)(2,1)} %reshape.427), calls=%async_computation.1 | async-start | bytes 147456 | tf_op jit(solution)/shard_map/all_to_all | solution.py:95
  40.3 1.9 copy.108
  42.5 6.3 %all-to-all-done.1 = bf16[16,2,1152]{2,1,0:T(2,128)(2,1)S(1)} async-done(((bf16[16,2,1152]{2,1,0:T(2,128)(2,1)}), bf16[16,2,1152]{2,1,0:T(2,128)(2,1)S(1)}, u32[]{:S(2)}, u32[]{:S(2)}) %all-to-all-start.1) | async-done | bytes 73760 | tf_op jit(solution)/shard_map/all_to_all | solution.py:95
  48.8 3.6 all-to-all-start.2
  52.4 27.4 %gather_fusion.1 = bf16[960,16,2,128]{3,2,1,0:T(2,128)(2,1)} fusion(bf16[528,16,2,128]{3,2,1,0:T(2,128)(2,1)} %param.16, s32[1024]{0:T(1024)S(1)} %pad_clamp_fusion.1), kind=kCustom, calls=%fused_computation.1 | custom fusion | bytes 15732480 | tf_op jit(solution)/shard_map/gather | solution.py:123
  79.8 7.3 %copy.105 = bf16[960,16,2,128]{3,1,2,0:T(8,128)(2,1)} copy(bf16[960,16,2,128]{3,2,1,0:T(2,128)(2,1)} %gather_fusion.1) | data formatting | bytes 15728640 | tf_op jit(solution)/shard_map/gather | solution.py:123
  87.2 0.1 multiply_cosine_fusion
  87.4 18.8 %all_gather.10 = bf16[128,2304]{0,1:T(8,128)(2,1)S(1)} all-gather(bf16[128,144]{0,1:T(8,128)(2,1)S(1)} %copy-done.2), channel_id=1, replica_groups=mesh['dp'=16,'fsdp'=16] {'dp'}, dimensions={1}, use_global_device_ids=true | all-gather | bytes 626688 | tf_op jit(solution)/shard_map/all_gather | solution.py:150
  106.3 0.1 convolution_convert_fusion.3
  106.4 0.2 fusion.3
  106.6 0.7 convolution_convert_fusion.5
  107.3 0.1 copy.110
  107.5 7.0 %pad_maximum_fusion = bf16[128,8,16,2,128]{4,2,3,1,0:T(8,128)(2,1)} fusion(bf16[8,8,16,2,128]{4,2,3,1,0:T(8,128)(2,1)S(1)} %copy.110, bf16[120,8,16,2,128]{4,2,3,1,0:T(8,128)(2,1)} %bitcast.89), kind=kLoop, calls=%fused_computation.3 | loop fusion | flops 4194304 | bytes 16777216 | tf_op jit(solution)/shard_map/concatenate | solution.py:124
  114.5 13.0 %copy.111 = bf16[128,8,16,2,128]{0,4,3,2,1:T(8,128)(2,1)} copy(bf16[128,8,16,2,128]{4,2,3,1,0:T(8,128)(2,1)} %pad_maximum_fusion) | data formatting | bytes 16777216 | tf_op jit(solution)/shard_map/concatenate | solution.py:124
  127.5 3.8 copy.103
  131.3 2.2 fusion.9
  133.6 3.9 multiply_reduce_fusion.1
  137.6 0.1 fusion.17
  137.7 0.2 fusion.18
  137.9 0.2 fusion.21
  138.2 3.2 multiply_reduce_fusion
  141.4 1.4 fusion.52
  143.0 0.6 dynamic-slice
  144.5 92.2 %all-reduce.3.cloned.1.call-done = f32[128,2304]{1,0:T(8,128)} async-done(((f32[128,2304]{1,0:T(8,128)}), f32[128,2304]{1,0:T(8,128)}) %all-reduce.3.cloned.1.call-update) | async-done | bytes 1179664
  236.6 1.0 multiply_reduce_fusion.2
  237.7 0.3 convolution_convert_fusion.1
  237.9 0.1 copy.112
  238.0 18.5 %all_to_all.50 = bf16[16,2,2304]{2,1,0:T(2,128)(2,1)} all-to-all(bf16[16,2,2304]{2,1,0:T(2,128)(2,1)S(1)} %copy.112), channel_id=1, replica_groups=mesh['dp'=16,'fsdp'=16] {'dp'}, dimensions={0} | all-to-all | bytes 294912 | tf_op jit(solution)/shard_map/all_to_all | solution.py:187
  256.5 5.1 %broadcast_in_dim.37 = bf16[8,2,144,2,360]{4,3,2,1,0:T(2,128)(2,1)} broadcast(bf16[8,144,2,360]{3,2,1,0:T(2,128)(2,1)} %param.22), dimensions={0,2,3,4} | broadcast | bytes 4976640 | tf_op jit(solution)/shard_map/broadcast_in_dim | solution.py:74
  261.6 4.5 all-to-all-start.4
  266.2 0.7 all-gather.6.cloned.1.call-update
  266.9 78.4 %all-to-all-done.4 = bf16[16,144,2,360]{3,2,1,0:T(2,128)(2,1)} async-done(((bf16[16,144,2,360]{3,2,1,0:T(2,128)(2,1)}), bf16[16,144,2,360]{3,2,1,0:T(2,128)(2,1)}, u32[]{:S(2)}, u32[]{:S(2)}) %all-to-all-start.4) | async-done | bytes 3317792 | tf_op jit(solution)/shard_map/all_to_all | solution.py:190
  345.3 1.4 broadcast_in_dim.38
  346.7 5.5 %all-to-all-start.5 = ((bf16[16,144,360]{2,1,0:T(8,128)(2,1)}), bf16[16,144,360]{2,1,0:T(8,128)(2,1)}, u32[]{:S(2)}, u32[]{:S(2)}) async-start(bf16[16,144,360]{2,1,0:T(8,128)(2,1)} %bitcast.32), calls=%async_computation.5 | async-start | bytes 3538944 | tf_op jit(solution)/shard_map/all_to_all | solution.py:191
  352.2 0.3 reduce-scatter.2.cloned.1.call-start
  352.5 8.5 %reshape_squeeze.3 = bf16[2304,720]{1,0:T(8,128)(2,1)} reshape(bf16[16,144,2,360]{3,2,1,0:T(2,128)(2,1)} %all-to-all-done.4) | data formatting | bytes 6635520 | tf_op jit(solution)/shard_map/reshape;squeeze | solution.py:195
  361.0 4.9 reshape.378
  365.9 5.1 %fusion.53 = f32[512,720]{0,1:T(8,128)} fusion(bf16[512,2304]{1,0:T(8,128)(2,1)S(1)} %reshape.378, bf16[2304,720]{1,0:T(8,128)(2,1)} %reshape_squeeze.3), kind=kOutput, calls=%fused_computation.133 | convolution fusion | flops 1698693120 | bytes 7151616 | tf_op jit(solution)/shard_map/dot_general | solution.py:197
  371.0 23.7 %all-to-all-done.5 = bf16[16,144,360]{2,1,0:T(8,128)(2,1)} async-done(((bf16[16,144,360]{2,1,0:T(8,128)(2,1)}), bf16[16,144,360]{2,1,0:T(8,128)(2,1)}, u32[]{:S(2)}, u32[]{:S(2)}) %all-to-all-start.5) | async-done | bytes 1658912 | tf_op jit(solution)/shard_map/all_to_all | solution.py:191
  394.7 4.9 convolution_convert_fusion
  399.6 0.2 fusion.50
  399.8 0.2 select_reduce_fusion.1
  399.9 74.2 %reduce-scatter.2.cloned.1.call-done = bf16[32,2304]{1,0:T(8,128)(2,1)} async-done(((bf16[512,2304]{1,0:T(8,128)(2,1)}), bf16[32,2304]{1,0:T(8,128)(2,1)}) %reduce-scatter.2.cloned.1.call-update) | async-done | bytes 147472 | tf_op jit(solution)/shard_map/reduce_scatter | solution.py:201
  474.1 1.8 reshape.385
  475.9 9.4 %all-to-all-start.6 = ((f32[16,2,2304]{2,1,0:T(2,128)}), f32[16,2,2304]{2,1,0:T(2,128)S(1)}, u32[]{:S(2)}, u32[]{:S(2)}) async-start(f32[16,2,2304]{2,1,0:T(2,128)} %reshape.385), calls=%async_computation.7 | async-start | bytes 589824 | tf_op jit(solution)/shard_map/all_to_all | solution.py:209
  485.4 12.2 %all-to-all-done.6 = f32[16,2,2304]{2,1,0:T(2,128)S(1)} async-done(((f32[16,2,2304]{2,1,0:T(2,128)}), f32[16,2,2304]{2,1,0:T(2,128)S(1)}, u32[]{:S(2)}, u32[]{:S(2)}) %all-to-all-start.6) | async-done | bytes 294944 | tf_op jit(solution)/shard_map/all_to_all | solution.py:209
  497.6 0.9 fusion.2
  (64 shorter events, 1.7 us)
Async XLA Ops:
  6.5 393.0 %copy-start = (bf16[2304,8]{0,1:T(8,128)(2,1)S(1)}, bf16[2304,8]{0,1:T(8,128)(2,1)}, u32[]{:S(2)}) copy-start(bf16[2304,8]{0,1:T(8,128)(2,1)} %param.21) | copy-start | bytes 110596
  6.5 120.9 %all-gather.4.cloned.1.call-start = ((), (), s32[]{:S(2)}) async-start(), calls=%async_computation.8 | async-start | bytes 1880064 | tf_op jit(solution)/shard_map/all_gather | solution.py:113
  8.9 18.7 %all-to-all-start = ((bf16[16,8,2304]{2,1,0:T(8,128)(2,1)}), bf16[16,8,2304]{2,1,0:T(8,128)(2,1)S(1)}, u32[]{:S(2)}, u32[]{:S(2)}) async-start(bf16[16,8,2304]{2,1,0:T(8,128)(2,1)} %stack.4), calls=%async_computation | async-start | bytes 1179648 | tf_op jit(solution)/shard_map/all_to_all | solution.py:12
  29.6 19.1 %all-to-all-start.1 = ((bf16[16,2,1152]{2,1,0:T(2,128)(2,1)}), bf16[16,2,1152]{2,1,0:T(2,128)(2,1)S(1)}, u32[]{:S(2)}, u32[]{:S(2)}) async-start(bf16[16,2,1152]{2,1,0:T(2,128)(2,1)} %reshape.427), calls=%async_computation.1 | async-start | bytes 147456 | tf_op jit(solution)/shard_map/all_to_all | solution.py:95
  48.8 57.8 %all-to-all-start.2 = ((bf16[16,8,16,2,128]{4,3,2,1,0:T(2,128)(2,1)}), bf16[16,8,16,2,128]{4,3,2,1,0:T(2,128)(2,1)S(1)}, u32[]{:S(2)}, u32[]{:S(2)}) async-start(bf16[16,8,16,2,128]{4,3,2,1,0:T(2,128)(2,1)} %copy.108), calls=%async_computation.2 | async-start | bytes 2097152 | tf_op jit(solution)/shard_map/all_to_all | solution.py:94
  52.3 184.3 %all-reduce.3.cloned.1.call-start = ((), (), s32[]{:S(2)}) async-start(), calls=%async_computation.11 | async-start | bytes 2359296
  79.8 7.3 %copy-start.4 = (bf16[2304]{0:T(1024)(128)(2,1)S(1)}, bf16[2304]{0:T(1024)(128)(2,1)}, u32[]{:S(2)}) copy-start(bf16[2304]{0:T(1024)(128)(2,1)} %param.19) | copy-start | bytes 13828
  79.8 7.6 %copy-start.2 = (bf16[128,144]{0,1:T(8,128)(2,1)S(1)}, bf16[128,144]{0,1:T(8,128)(2,1)}, u32[]{:S(2)}) copy-start(bf16[128,144]{0,1:T(8,128)(2,1)} %param.18) | copy-start | bytes 110596
  141.4 1.5 copy-start.3
  141.4 1.6 copy-start.5
  141.4 1.6 copy-start.6
  261.6 83.7 %copy-start.1 = (bf16[8,144,360]{2,1,0:T(8,128)(2,1)S(1)}, bf16[8,144,360]{2,1,0:T(8,128)(2,1)}, u32[]{:S(2)}) copy-start(bf16[8,144,360]{2,1,0:T(8,128)(2,1)} %param.23) | copy-start | bytes 2488324
  261.6 83.7 %all-to-all-start.4 = ((bf16[16,144,2,360]{3,2,1,0:T(2,128)(2,1)}), bf16[16,144,2,360]{3,2,1,0:T(2,128)(2,1)}, u32[]{:S(2)}, u32[]{:S(2)}) async-start(bf16[16,144,2,360]{3,2,1,0:T(2,128)(2,1)} %bitcast.90), calls=%async_computation.4 | async-start | bytes 7077888 | tf_op jit(solution)/shard_map/all_to_all | solution.py:190
  266.2 94.8 %all-gather.6.cloned.1.call-start = ((), (), s32[]{:S(2)}) async-start(), calls=%async_computation.10 | async-start | bytes 2506752 | tf_op jit(solution)/shard_map/all_gather | solution.py:188
  346.7 48.0 %all-to-all-start.5 = ((bf16[16,144,360]{2,1,0:T(8,128)(2,1)}), bf16[16,144,360]{2,1,0:T(8,128)(2,1)}, u32[]{:S(2)}, u32[]{:S(2)}) async-start(bf16[16,144,360]{2,1,0:T(8,128)(2,1)} %bitcast.32), calls=%async_computation.5 | async-start | bytes 3538944 | tf_op jit(solution)/shard_map/all_to_all | solution.py:191
  352.2 121.9 %reduce-scatter.2.cloned.1.call-start = ((), (), s32[]{:S(2)}) async-start(), calls=%async_computation.9 | async-start | bytes 2506752 | tf_op jit(solution)/shard_map/reduce_scatter | solution.py:201
  475.9 21.7 %all-to-all-start.6 = ((f32[16,2,2304]{2,1,0:T(2,128)}), f32[16,2,2304]{2,1,0:T(2,128)S(1)}, u32[]{:S(2)}, u32[]{:S(2)}) async-start(f32[16,2,2304]{2,1,0:T(2,128)} %reshape.385), calls=%async_computation.7 | async-start | bytes 589824 | tf_op jit(solution)/shard_map/all_to_all | solution.py:209
Sparse Core Ops, SparseCore 0:
  9.2 43.4 all-gather.3
  143.0 93.6 all-reduce.2
  269.4 48.1 all-gather.5
  399.7 74.3 reduce-scatter.1
